TPU v7x, 256 devices: a whole 4x4x8 slice. The times are simulated.
256 devices in a mesh: space: 64 (over z, x, core), inst: 4 (over y).
Axes of the slice: x: 4, y: 4, z: 8, core: 2. Of those that a mesh axis runs over, the one named last changes fastest.
Arguments:
- adjoint: float32 [8, 5, 131072], P('inst', None, 'space'), may hold values from -6 to 6
- jac_cell: float32 [8, 5, 5, 131072], P('inst', None, None, 'space'), may hold values from -2.5 to 2.5
- jac_left: float32 [8, 5, 5, 131072], P('inst', None, None, 'space'), may hold values from -2.5 to 2.5
- jac_right: float32 [8, 5, 5, 131072], P('inst', None, None, 'space'), may hold values from -2.5 to 2.5
- volume: float32 [131072], P('space'), may hold values from 0.5 to 2
- normals: float32 [3, 131072], P(None, 'space'), may hold values from -6 to 6
- surface: int32 [131072], P('space'), may hold values 0 or 1
- instance_map: int32 [8], replicated, may hold values from 0 to 7, each once
- mode_shapes: float32 [200, 3, 131072], P(None, None, 'space'), may hold values from -0.01953125 to 0.01953125
- damping: float32 [200], replicated, may hold values from 0.2 to 2
- modal_inverse: float32 [200, 200], replicated, may hold values from -2 to 3
Outputs:
- flow_residual: float32 [8, 5, 131072], P('inst', None, 'space')
- mesh_forcing: float32 [8, 3, 131072], P('inst', None, 'space')
- modal_adjoint: float32 [8, 200], P('inst')
All inputs are finite; a program needn't handle non-finite values. No bound on the sum of `surface` on one device may be relied on, other than what follows from the above.
Results may differ from a plain program's by a relative error of at most 0.000068.
Values sent between devices are 32-bit elements; how exact they have to be, the bound alone decides.
A program may use at most 64 MiB of HBM per device.

v0:
```python
import jax
import jax.numpy as jnp
from jax import lax
from jax.sharding import PartitionSpec as P


def padded_2(shard, sides, width):
    for axis, dim in sides:
        count, length = (lax.axis_size(axis), shard.shape[dim])
        up = [(i, (i + 1) % count) for i in range(count - 1)]
        down = [(j, i) for i, j in up]
        last = lax.slice_in_dim(shard, length - width, length, axis=dim)
        leading = lax.slice_in_dim(shard, 0, width, axis=dim)
        before = lax.ppermute(last, axis, up)
        after = lax.ppermute(leading, axis, down)
        shard = jnp.concatenate([before, shard, after], axis=dim)
    return shard


def coupling_matrix(instance_map):
    count = instance_map.shape[0]
    slots = instance_map.astype(jnp.float32)
    differ = slots[:, None] - slots[None, :]
    angle = jnp.pi * differ / count
    same = differ == 0
    sine = jnp.where(same, 1.0, jnp.sin(angle))
    return jnp.where(same, 0.0, 0.5 * jnp.cos(jnp.pi * differ) * jnp.cos(angle) / sine)


def shards(
    adjoint,
    jac_cell,
    jac_left,
    jac_right,
    volume,
    normals,
    surface,
    instance_map,
    mode_shapes,
    damping,
    modal_inverse,
):
    highest = lax.Precision.HIGHEST
    own_slots = adjoint.shape[0]
    modes = mode_shapes.shape[0]
    first_slot = lax.axis_index("inst") * own_slots
    coupling = coupling_matrix(instance_map)
    own_cols = lax.dynamic_slice_in_dim(coupling, first_slot, own_slots, 1)
    flow = jnp.einsum("sfec,sfc->sec", jac_cell, adjoint, precision=highest)
    from_left = jnp.einsum("sfec,sfc->sec", jac_left, adjoint, precision=highest)
    from_right = jnp.einsum("sfec,sfc->sec", jac_right, adjoint, precision=highest)
    stacked = jnp.stack([from_left, from_right])
    padded = padded_2(stacked, (("space", 3),), 1)
    flow = flow + padded[0, :, :, 2:] + padded[1, :, :, :-2]
    timed = jnp.einsum(
        "ab,aec->bec",
        own_cols,
        lax.all_gather(adjoint, "inst", axis=0, tiled=True),
        precision=highest,
    )
    flow = flow + volume[None, None, :] * timed
    walls = surface.astype(jnp.float32)
    force = (walls[None, :] * flow[:, 4, :])[:, None, :] * normals[None, :, :]
    shapes = mode_shapes.reshape(modes, -1)
    projected = lax.dot_general(
        force.reshape(own_slots, -1),
        shapes,
        (((1,), (1,)), ((), ())),
        precision=highest,
        preferred_element_type=jnp.float32,
    )
    summed = lax.psum(projected, "space")
    gathered = lax.all_gather(summed, "inst", axis=0, tiled=True)
    own_projected = lax.dynamic_slice_in_dim(gathered, first_slot, own_slots, 0)
    modal_rhs = own_projected + damping[None, :] * jnp.dot(own_cols.T, gathered, precision=highest)
    modal_adjoint = jnp.dot(modal_rhs, modal_inverse, precision=highest)
    expanded = jnp.dot(modal_adjoint, shapes, precision=highest).reshape(own_slots, 3, -1)
    mesh_forcing = walls[None, None, :] * expanded
    return (flow, mesh_forcing, modal_adjoint)


def solution(mesh):
    placed = (
        P("inst", None, "space"),
        P("inst", None, None, "space"),
        P("inst", None, None, "space"),
        P("inst", None, None, "space"),
        P("space"),
        P(None, "space"),
        P("space"),
        P(),
        P(None, None, "space"),
        P(),
        P(),
    )
    return jax.shard_map(
        shards,
        mesh=mesh,
        in_specs=placed,
        out_specs=(P("inst", None, "space"), P("inst", None, "space"), P("inst", None)),
        check_vma=False,
    )
```

profile of v0, /device:TPU:8, one launch (start us, length us, event | category | flops | bytes accessed | tf_op | source)
XLA Modules:
  0.0 175.6 jit_solution(5606615448060914393)
XLA Ops:
  0.6 0.0 copy-start
  0.6 0.0 copy-start.3
  0.7 2.1 %multiply_reduce_fusion.2 = (f32[2,2048,5]{1,0,2:T(2,128)S(1)}, f32[2,2048,5]{1,0,2:T(2,128)S(1)}, f32[2,2048,5]{1,0,2:T(2,128)S(1)}) fusion(f32[2,5,5,2048]{3,0,2,1:T(2,128)} %param.12, f32[2,2048,5]{1,0,2:T(2,128)} %bitcast.61, f32[2,5,5,2048]{3,0,2,1:T(2,128)} %param.13, f32[2,5,5,2048]{3,0,2,1:T(2,128)} %param.14), kind=kLoop, calls=%fused_computation.10 | loop fusion | flops 552960 | bytes 1556480 | tf_op jit(solution)/shard_map/sfec,sfc->sec/dot_general | solution.py:49
  2.8 0.1 pad_maximum_fusion.5
  2.9 1.7 collective-permute-start.1
  4.6 1.3 collective-permute-start
  5.9 0.9 copy.16
  6.8 13.6 %all_gather.6 = f32[8,5,2048]{2,1,0:T(8,128)S(1)} all-gather(f32[2,5,2048]{2,1,0:T(8,128)S(1)} %copy.16), channel_id=1, replica_groups=mesh['space'=64,'inst'=4] {'inst'}, dimensions={0}, use_global_device_ids=true | all-gather | bytes 409600 | tf_op jit(solution)/shard_map/all_gather | solution.py:58
  20.5 0.7 convert_element_type.6
  21.1 0.1 fusion.21
  21.3 0.7 convert_element_type.7
  22.0 0.0 collective-permute-done.1
  22.0 0.0 collective-permute-done
  22.0 1.3 fusion.10
  23.3 0.0 copy-start.2
  23.3 5.8 %convolution_bitcast_fusion = f32[2,200]{1,0:T(2,128)S(1)} fusion(f32[200,3,2048]{2,0,1:T(8,128)} %param.19, f32[3,2048]{1,0:T(4,128)} %param.16, f32[2,2048]{1,0:T(2,128)S(1)} %fusion.18), kind=kOutput, calls=%fused_computation.6 | convolution fusion | flops 29503488 | bytes 4957760 | tf_op jit(solution)/shard_map/dot_general | solution.py:65
  29.1 129.9 %psum.7 = f32[2,200]{1,0:T(2,128)S(1)} all-reduce(f32[2,200]{1,0:T(2,128)S(1)} %convolution_bitcast_fusion), channel_id=1, replica_groups=mesh['space'=64,'inst'=4] {'space'}, use_global_device_ids=true, to_apply=%region_0.1 | all-reduce | flops 400 | bytes 3200 | tf_op jit(solution)/shard_map/psum | solution.py:72
  159.1 10.7 %all-gather = f32[4,2,200]{2,1,0:T(2,128)S(1)} all-gather(f32[1,2,200]{2,1,0:T(2,128)S(1)} %bitcast.66), channel_id=1, replica_groups=mesh['space'=64,'inst'=4] {'inst'}, dimensions={0}, use_global_device_ids=true | all-gather | bytes 8000 | tf_op jit(solution)/shard_map/all_gather | solution.py:73
  169.8 0.0 copy-done.3
  169.8 0.1 fusion.6
  169.9 0.0 copy-done
  169.9 0.2 fusion.33
  170.1 0.0 copy-start.1
  170.1 5.5 %fusion.3 = f32[2,3,2048]{2,0,1:T(2,128)} fusion(f32[2048]{0:T(1024)S(1)} %convert_element_type.7, f32[2,200]{1,0:T(2,128)S(1)} %fusion.33, f32[200,3,2048]{2,0,1:T(8,128)} %param.19), kind=kOutput, calls=%fused_computation.4 | convolution fusion | flops 29503488 | bytes 4974144 | tf_op jit(solution)/shard_map/dot_general | solution.py:77
  175.6 0.0 copy-done.2
  175.6 0.0 copy-done.1
  (2 shorter events, 0.0 us)
Async XLA Ops:
  0.6 169.3 %copy-start = (f32[200,200]{1,0:T(8,128)S(1)}, f32[200,200]{1,0:T(8,128)}, u32[]{:S(2)}) copy-start(f32[200,200]{1,0:T(8,128)} %param.21) | copy-start | bytes 480004
  0.6 169.1 %copy-start.3 = (f32[200]{0:T(256)S(1)}, f32[200]{0:T(256)}, u32[]{:S(2)}) copy-start(f32[200]{0:T(256)} %param.20) | copy-start | bytes 2404
  2.9 19.1 %collective-permute-start.1 = (f32[2,2,5,1]{3,1,2,0:T(2,128)S(1)}, f32[2,2,5,1]{3,1,2,0:T(2,128)S(1)}, u32[]{:S(2)}, u32[]{:S(2)}) collective-permute-start(f32[2,2,5,1]{3,1,2,0:T(2,128)S(1)} %get-tuple-element.7), channel_id=1, source_target_pairs={{0,4},{4,8},{8,12},{12,16},{16,20},{20,24},{24,28},{28,32},{32,36}... | collective-permute-start | bytes 248 | tf_op jit(solution)/shard_map/ppermute | solution.py:14
  4.6 17.4 %collective-permute-start = (f32[2,2,5,1]{3,1,2,0:T(2,128)S(1)}, f32[2,2,5,1]{3,1,2,0:T(2,128)S(1)}, u32[]{:S(2)}, u32[]{:S(2)}) collective-permute-start(f32[2,2,5,1]{3,1,2,0:T(2,128)S(1)} %get-tuple-element.6), channel_id=1, source_target_pairs={{4,0},{8,4},{12,8},{16,12},{20,16},{24,20},{28,24},{32,28},{36,32}... | collective-permute-start | bytes 248 | tf_op jit(solution)/shard_map/ppermute | solution.py:15
  23.3 152.3 %copy-start.2 = (f32[2,5,2048]{2,0,1:T(2,128)}, f32[2,5,2048]{2,0,1:T(2,128)S(1)}, u32[]{:S(2)}) copy-start(f32[2,5,2048]{2,0,1:T(2,128)S(1)} %fusion.10) | copy-start | bytes 245764
  170.1 5.5 %copy-start.1 = (f32[2,200]{1,0:T(2,128)}, f32[2,200]{1,0:T(2,128)S(1)}, u32[]{:S(2)}) copy-start(f32[2,200]{1,0:T(2,128)S(1)} %fusion.33) | copy-start | bytes 4804
where the time goes:
time: 176 us
  blocking collectives  154 us (88%)
  matrix products  12.8 us (7%)
  other arithmetic  3.69 us (2%)
  starting transfers between devices  3.02 us (2%)
    psum x1, blocking collectives, shards(): summed = lax.psum(projected, 'space')  130 us
    all_gather x1, blocking collectives, shards(): lax.all_gather(adjoint, 'inst', axis=0, tiled=True)  13.6 us
    all_gather x1, blocking collectives, shards(): gathered = lax.all_gather(summed, 'inst', axis=0, tiled=True)  10.7 us
    dot_general x1, matrix products, shards(): lax.dot_general(force.reshape(own_slots, -1), shapes, (((1,), (1,)), ((),...  5.76 us
    dot_general x1, matrix products, shards(): jnp.dot(modal_adjoint, shapes, precision=highest).reshape(own_slots, 3, -1)  5.45 us
  transfers between devices with their start and end apart: 2, of which 0 were waited for; matrix products, arithmetic and copies ran while one was open for 1% of the time, Pallas kernels for 0%

commit v1 on v0

--- a/solution.py
+++ b/solution.py
@@ -52,12 +52,32 @@
     stacked = jnp.stack([from_left, from_right])
     padded = padded_2(stacked, (("space", 3),), 1)
     flow = flow + padded[0, :, :, 2:] + padded[1, :, :, :-2]
+    tall, block_out = (lax.axis_size("inst"), lax.axis_index("inst"))
+    bank = []
+    dev_i = 0
+    while dev_i < tall:
+        bank.append((dev_i, (dev_i - 1) % tall))
+        dev_i = dev_i + 1
+    formed = adjoint.shape[0]
+    known = adjoint
     timed = jnp.einsum(
         "ab,aec->bec",
-        own_cols,
-        lax.all_gather(adjoint, "inst", axis=0, tiled=True),
+        lax.dynamic_slice_in_dim(own_cols, block_out * formed, known.shape[0], axis=0),
+        known,
         precision=highest,
     )
+    dev = 1
+    while dev < tall:
+        known = lax.ppermute(known, "inst", bank)
+        timed = timed + jnp.einsum(
+            "ab,aec->bec",
+            lax.dynamic_slice_in_dim(
+                own_cols, (block_out + dev) % tall * formed, known.shape[0], axis=0
+            ),
+            known,
+            precision=highest,
+        )
+        dev += 1
     flow = flow + volume[None, None, :] * timed
     walls = surface.astype(jnp.float32)
     force = (walls[None, :] * flow[:, 4, :])[:, None, :] * normals[None, :, :]

time: 176 us -> 176 us (level)
  blocking collectives: 154 us -> 142 us
  waiting for transfers between devices: 0.01 us -> 6.53 us
  starting transfers between devices: 3.02 us -> 7.02 us
  matrix products: 12.8 us -> 15.1 us
    all_gather x1 -> x0, blocking collectives: 13.6 us -> none  [shards(): lax.all_gather(adjoint, 'inst', axis=0, tiled=True)]
    ppermute x0 -> x3, waiting for transfers between devices: none -> 6.52 us  [shards(): known = lax.ppermute(known, 'inst', bank)]
    ppermute x0 -> x3, starting transfers between devices: none -> 4.45 us  [shards(): known = lax.ppermute(known, 'inst', bank)]
    dot_general x1 -> x4, matrix products: 1.31 us -> 3.54 us  [the longest x3 2.18 us: shards(): jnp.einsum('ab,aec->bec', lax.dynamic_slice_in_dim(own_cols, (block_out +...]
    all_gather x1, blocking collectives: 10.7 us -> 12.7 us  [shards(): gathered = lax.all_gather(summed, 'inst', axis=0, tiled=True)]
  transfers between devices with their start and end apart: 2 -> 5, of which waited for: 0 -> 2; matrix products, arithmetic and copies ran while one was open for 1% -> 3% of each run, Pallas kernels for 0% -> 0%
where the time goes in v1:
time: 176 us; the launch traced here: 175 us
  blocking collectives  142 us (81%)
  matrix products  15.1 us (9%)
  starting transfers between devices  7.02 us (4%)
  waiting for transfers between devices  6.53 us (4%)
  other arithmetic  3.69 us (2%)
    psum x1, blocking collectives, shards(): summed = lax.psum(projected, 'space')  130 us
    all_gather x1, blocking collectives, shards(): gathered = lax.all_gather(summed, 'inst', axis=0, tiled=True)  12.7 us
    ppermute x3, waiting for transfers between devices, shards(): known = lax.ppermute(known, 'inst', bank)  6.52 us
    dot_general x1, matrix products, shards(): lax.dot_general(force.reshape(own_slots, -1), shapes, (((1,), (1,)), ((),...  5.76 us
    dot_general x1, matrix products, shards(): jnp.dot(modal_adjoint, shapes, precision=highest).reshape(own_slots, 3, -1)  5.45 us
    ppermute x3, starting transfers between devices, shards(): known = lax.ppermute(known, 'inst', bank)  4.45 us
  transfers between devices with their start and end apart: 5, of which 2 were waited for; matrix products, arithmetic and copies ran while one was open for 3% of the time, Pallas kernels for 0%

profile of v1, /device:TPU:8, one launch (start us, length us, event | category | flops | bytes accessed | tf_op | source)
XLA Modules:
  0.0 175.4 jit_solution(5982157432668248277)
XLA Ops:
  0.6 0.0 copy-start
  0.6 0.0 copy-start.3
  0.7 2.3 %collective-permute-start.2 = (f32[2,5,2048]{2,0,1:T(2,128)}, f32[2,5,2048]{2,0,1:T(2,128)S(1)}, u32[]{:S(2)}, u32[]{:S(2)}) collective-permute-start(f32[2,5,2048]{2,0,1:T(2,128)} %param.11), channel_id=1, source_target_pairs={{0,3},{1,0},{2,1},{3,2},{4,7},{5,4},{6,5},{7,6},{8,11},{9,8},{10,9... | collective-permute-start | bytes 245768 | tf_op jit(solution)/shard_map/ppermute | solution.py:71
  2.9 2.1 %multiply_reduce_fusion.2 = (f32[2,2048,5]{1,0,2:T(2,128)S(1)}, f32[2,2048,5]{1,0,2:T(2,128)S(1)}, f32[2,2048,5]{1,0,2:T(2,128)S(1)}) fusion(f32[2,5,5,2048]{3,0,2,1:T(2,128)} %param.12, f32[2,2048,5]{1,0,2:T(2,128)} %bitcast.74, f32[2,5,5,2048]{3,0,2,1:T(2,128)} %param.13, f32[2,5,5,2048]{3,0,2,1:T(2,128)} %param.14), kind=kLoop, calls=%fused_computation.14 | loop fusion | flops 552960 | bytes 1556480 | tf_op jit(solution)/shard_map/sfec,sfc->sec/dot_general | solution.py:49
  5.0 0.1 pad_maximum_fusion.5
  5.1 1.3 collective-permute-start.1
  6.4 1.3 collective-permute-start
  7.7 0.7 convert_element_type.6
  8.4 0.1 fusion.19
  8.5 1.4 fusion.29
  9.9 0.7 convert_element_type.7
  10.6 0.0 collective-permute-done.2
  10.6 1.4 collective-permute-start.3
  12.1 0.5 convolution_add_fusion.2
  12.6 3.2 %collective-permute-done.3 = f32[2,5,2048]{2,0,1:T(2,128)S(1)} collective-permute-done((f32[2,5,2048]{2,0,1:T(2,128)S(1)}, f32[2,5,2048]{2,0,1:T(2,128)S(1)}, u32[]{:S(2)}, u32[]{:S(2)}) %collective-permute-start.3) | collective-permute-done | bytes 81952 | tf_op jit(solution)/shard_map/ppermute | solution.py:71
  15.8 0.7 collective-permute-start.4
  16.5 0.5 convolution_add_fusion.1
  17.0 0.0 collective-permute-done.1
  17.0 0.0 collective-permute-done
  17.0 3.3 %collective-permute-done.4 = f32[2,5,2048]{2,0,1:T(2,128)S(1)} collective-permute-done((f32[2,5,2048]{2,0,1:T(2,128)S(1)}, f32[2,5,2048]{2,0,1:T(2,128)S(1)}, u32[]{:S(2)}, u32[]{:S(2)}) %collective-permute-start.4) | collective-permute-done | bytes 81952 | tf_op jit(solution)/shard_map/ppermute | solution.py:71
  20.3 1.2 fusion.4
  21.6 0.0 copy-start.2
  21.6 5.8 %convolution_bitcast_fusion = f32[2,200]{1,0:T(2,128)S(1)} fusion(f32[200,3,2048]{2,0,1:T(8,128)} %param.19, f32[3,2048]{1,0:T(4,128)} %param.16, f32[2,2048]{1,0:T(2,128)S(1)} %fusion.16), kind=kOutput, calls=%fused_computation.10 | convolution fusion | flops 29503488 | bytes 4957760 | tf_op jit(solution)/shard_map/dot_general | solution.py:85
  27.4 129.5 %psum.7 = f32[2,200]{1,0:T(2,128)S(1)} all-reduce(f32[2,200]{1,0:T(2,128)S(1)} %convolution_bitcast_fusion), channel_id=1, replica_groups=mesh['space'=64,'inst'=4] {'space'}, use_global_device_ids=true, to_apply=%region_0.1 | all-reduce | flops 400 | bytes 3200 | tf_op jit(solution)/shard_map/psum | solution.py:92
  156.9 12.7 %all-gather = f32[4,2,200]{2,1,0:T(2,128)S(1)} all-gather(f32[1,2,200]{2,1,0:T(2,128)S(1)} %bitcast.79), channel_id=1, replica_groups=mesh['space'=64,'inst'=4] {'inst'}, dimensions={0}, use_global_device_ids=true | all-gather | bytes 8000 | tf_op jit(solution)/shard_map/all_gather | solution.py:93
  169.6 0.0 copy-done.3
  169.6 0.1 fusion.8
  169.8 0.0 copy-done
  169.8 0.2 fusion.37
  170.0 0.0 copy-start.1
  170.0 5.5 %fusion.5 = f32[2,3,2048]{2,0,1:T(2,128)} fusion(f32[2048]{0:T(1024)S(1)} %convert_element_type.7, f32[2,200]{1,0:T(2,128)S(1)} %fusion.37, f32[200,3,2048]{2,0,1:T(8,128)} %param.19), kind=kOutput, calls=%fused_computation.8 | convolution fusion | flops 29503488 | bytes 4974144 | tf_op jit(solution)/shard_map/dot_general | solution.py:97
  175.4 0.0 copy-done.2
  175.4 0.0 copy-done.1
  (2 shorter events, 0.0 us)
Async XLA Ops:
  0.6 169.1 %copy-start = (f32[200,200]{1,0:T(8,128)S(1)}, f32[200,200]{1,0:T(8,128)}, u32[]{:S(2)}) copy-start(f32[200,200]{1,0:T(8,128)} %param.21) | copy-start | bytes 480004
  0.6 169.0 %copy-start.3 = (f32[200]{0:T(256)S(1)}, f32[200]{0:T(256)}, u32[]{:S(2)}) copy-start(f32[200]{0:T(256)} %param.20) | copy-start | bytes 2404
  0.7 10.0 %collective-permute-start.2 = (f32[2,5,2048]{2,0,1:T(2,128)}, f32[2,5,2048]{2,0,1:T(2,128)S(1)}, u32[]{:S(2)}, u32[]{:S(2)}) collective-permute-start(f32[2,5,2048]{2,0,1:T(2,128)} %param.11), channel_id=1, source_target_pairs={{0,3},{1,0},{2,1},{3,2},{4,7},{5,4},{6,5},{7,6},{8,11},{9,8},{10,9... | collective-permute-start | bytes 245768 | tf_op jit(solution)/shard_map/ppermute | solution.py:71
  5.1 11.9 %collective-permute-start.1 = (f32[2,2,5,1]{3,1,2,0:T(2,128)S(1)}, f32[2,2,5,1]{3,1,2,0:T(2,128)S(1)}, u32[]{:S(2)}, u32[]{:S(2)}) collective-permute-start(f32[2,2,5,1]{3,1,2,0:T(2,128)S(1)} %get-tuple-element.7), channel_id=1, source_target_pairs={{0,4},{4,8},{8,12},{12,16},{16,20},{20,24},{24,28},{28,32},{32,36}... | collective-permute-start | bytes 248 | tf_op jit(solution)/shard_map/ppermute | solution.py:14
  6.4 10.6 %collective-permute-start = (f32[2,2,5,1]{3,1,2,0:T(2,128)S(1)}, f32[2,2,5,1]{3,1,2,0:T(2,128)S(1)}, u32[]{:S(2)}, u32[]{:S(2)}) collective-permute-start(f32[2,2,5,1]{3,1,2,0:T(2,128)S(1)} %get-tuple-element.6), channel_id=1, source_target_pairs={{4,0},{8,4},{12,8},{16,12},{20,16},{24,20},{28,24},{32,28},{36,32}... | collective-permute-start | bytes 248 | tf_op jit(solution)/shard_map/ppermute | solution.py:15
  10.6 5.2 %collective-permute-start.3 = (f32[2,5,2048]{2,0,1:T(2,128)S(1)}, f32[2,5,2048]{2,0,1:T(2,128)S(1)}, u32[]{:S(2)}, u32[]{:S(2)}) collective-permute-start(f32[2,5,2048]{2,0,1:T(2,128)S(1)} %collective-permute-done.2), channel_id=1, source_target_pairs={{0,3},{1,0},{2,1},{3,2},{4,7},{5,4},{6,5},{7,6},{8,11},{9,8},{10,9... | collective-permute-start | bytes 245768 | tf_op jit(solution)/shard_map/ppermute | solution.py:71
  15.8 4.5 %collective-permute-start.4 = (f32[2,5,2048]{2,0,1:T(2,128)S(1)}, f32[2,5,2048]{2,0,1:T(2,128)S(1)}, u32[]{:S(2)}, u32[]{:S(2)}) collective-permute-start(f32[2,5,2048]{2,0,1:T(2,128)S(1)} %collective-permute-done.3), channel_id=1, source_target_pairs={{0,3},{1,0},{2,1},{3,2},{4,7},{5,4},{6,5},{7,6},{8,11},{9,8},{10,9... | collective-permute-start | bytes 245768 | tf_op jit(solution)/shard_map/ppermute | solution.py:71
  21.6 153.9 %copy-start.2 = (f32[2,5,2048]{2,0,1:T(2,128)}, f32[2,5,2048]{2,0,1:T(2,128)S(1)}, u32[]{:S(2)}) copy-start(f32[2,5,2048]{2,0,1:T(2,128)S(1)} %fusion.4) | copy-start | bytes 245764
  170.0 5.5 %copy-start.1 = (f32[2,200]{1,0:T(2,128)}, f32[2,200]{1,0:T(2,128)S(1)}, u32[]{:S(2)}) copy-start(f32[2,200]{1,0:T(2,128)S(1)} %fusion.37) | copy-start | bytes 4804
